TPU v7x, 32 devices: a whole 2x2x4 slice. The times are simulated.
32 devices in a mesh: groups: 2 (over y), row: 4 (over x, core), col: 4 (over z).
Axes of the slice: x: 2, y: 2, z: 4, core: 2. Of those that a mesh axis runs over, the one named last changes fastest.
Arguments:
- inputs: bfloat16 [1536, 4096], P(('groups', 'col'), 'row'), parts along dimension 0, may hold values from -6 to 6
- cotangent: bfloat16 [1536, 4096], P(('groups', 'col'), 'row'), parts along dimension 0, may hold values from -6 to 6
- preactivation: bfloat16 [1536, 8192], P(('groups', 'row'), 'col'), parts along dimension 0, may hold values from -8 to 8
- up_weight: bfloat16 [4096, 8192], P('row', 'col'), may hold values from -0.09375 to 0.09375
- down_weight: bfloat16 [8192, 4096], P('col', 'row'), may hold values from -0.0625 to 0.0625
Outputs:
- grad_input: bfloat16 [1536, 4096], P(('groups', 'col'), 'row'), parts along dimension 0
- grad_up: float32 [8192, 8192], P(('groups', 'row'), 'col'), parts along dimension 0
- grad_down: float32 [16384, 4096], P(('groups', 'col'), 'row'), parts along dimension 0
There are 2 independent parts, one for each index of `groups`. A program takes and returns all parts, laid end to end along the dimension named above; an argument that names none is the same for every part. Nothing has to cross between parts.
All inputs are finite; a program needn't handle non-finite values.
Results may differ from a plain program's by a relative error of at most 0.0049.
Values may be sent and summed in bfloat16 or wider, within the bound.
A program may use at most 128 MiB of HBM per device.

v0:
```python
import functools
import math

import jax
import jax.numpy as jnp
from jax import lax
from jax.experimental import pallas as pl
from jax.experimental.pallas import tpu as pltpu
from jax.sharding import PartitionSpec as P

F32, BF16 = jnp.float32, jnp.bfloat16
LAST = (((1,), (1,)), ((), ()))
FIRST = (((0,), (0,)), ((), ()))


def tanh_of(v):
    return jnp.tanh(0.7978845608 * (v + 0.044715 * v * v * v))


def gelu_value(values):
    v = values.astype(F32)
    return 0.5 * v * (1.0 + tanh_of(v))


def gelu_pair(values):
    v = values.astype(F32)
    t = tanh_of(v)
    slope = 0.5 * (1.0 + t) + 0.5 * v * (1.0 - t * t) * 0.7978845608 * (1.0 + 3.0 * 0.044715 * v * v)
    return 0.5 * v * (1.0 + t), slope


def remote(src, dst, send, recv, where):
    return pltpu.make_async_remote_copy(
        src_ref=src, dst_ref=dst, send_sem=send, recv_sem=recv, device_id=where,
        device_id_type=pl.DeviceIdType.MESH,
    )


def pick(table, c):
    value = table[0]
    for at, other in enumerate(table):
        if at > 0:
            value = jnp.where(c == at, other, value)
    return value


def visit_order(nc):
    orders = []
    for c in range(nc):
        far = [(j, c, j) if j > c else (nc - 1 - j, nc - 1 - c, j) for j in range(nc) if j != c]
        orders.append([j for _, _, j in sorted(far)])
    return orders


def block_at(c, t, nc):
    near = jnp.minimum(c, nc - 1 - c)
    step = -((t + 1) // 2) if t % 2 else t // 2
    return jnp.where(t <= 2 * near, c + step, jnp.where(2 * c < nc - 1, t, nc - 1 - t))


def kernel(
    nr, nc,
    x_ref, cot_ref, pre_ref, up_ref, down_ref,
    *rest,
):
    gi_ref, x_out, pg_out, gd_out = rest[:4]
    (
    x_all, cot_all, pre_all, act_all, pg_all, up, down, part, h1_out, h1_in, h2_out, h2_in,
    gi_own, gi_acc, gi_out, gi_in, gd_buf,
    loc, cot_s, cot_r, x_s, x_r, pre_s, pre_on, pre_r, h1_s, h1_r, h2_s, h2_r, pg_s, pg_r, gi_s, gi_r,
    x_o, pg_o, gd_o,
    ) = rest[4:]
    r, c = lax.axis_index("row"), lax.axis_index("col")
    nx = nr // 2
    x, k = r // 2, r % 2
    mate_row = 2 * x + (1 - k)
    mate = {"row": mate_row}
    tb, dr = x_ref.shape
    ts, hc = pg_all.shape[1:]
    nq, dq = gi_out.shape[1], gi_out.shape[3]
    hb, eb, gb = min(512, hc), min(256, hc), gd_buf.shape[1]
    peers = [(x + d) % nx for d in range(1, nx)]
    token_scale = 1.0 / math.sqrt(tb * nc)
    end = (c == 0) | (c == nc - 1)
    ends = []

    barrier = pltpu.get_barrier_semaphore()
    for d in range(1, nr):
        pl.semaphore_signal(barrier, inc=1, device_id={"row": (r + d) % nr}, device_id_type=pl.DeviceIdType.MESH)
    for d in range(1, nc):
        pl.semaphore_signal(barrier, inc=1, device_id={"col": (c + d) % nc}, device_id_type=pl.DeviceIdType.MESH)
    local = [
        pltpu.make_async_copy(cot_ref, cot_all.at[c], loc.at[0]),
        pltpu.make_async_copy(down_ref, down, loc.at[1]),
        pltpu.make_async_copy(pre_ref, pre_all.at[pl.ds(r * nc, nc)], loc.at[2]),
        pltpu.make_async_copy(up_ref, up, loc.at[3]),
        pltpu.make_async_copy(x_ref, x_all.at[c], loc.at[4]),
    ]
    for copy in local:
        copy.start()
    pl.semaphore_wait(barrier, nr + nc - 2)

    def started(copy):
        copy.start()
        ends.append(copy)

    def line(all_ref, send, recv, direction, j, source):
        return remote(source, all_ref.at[j], send.at[direction, j], recv.at[j],
                      {"col": c + 1 if direction == 0 else c - 1})

    def pass_on(all_ref, send, recv, own_ref, t):
        for direction, j in ((0, c - t), (1, c + t)):
            there = (j >= 0) & (j < nc)
            onward = (c + 1 < nc) if direction == 0 else (c >= 1)
            jj = jnp.clip(j, 0, nc - 1)
            if t > 0:
                @pl.when(there)
                def _():
                    line(all_ref, send, recv, direction, jj, all_ref.at[jj]).wait_recv()

            @pl.when(there & onward)
            def _():
                src = own_ref if t == 0 else all_ref.at[jj]
                line(all_ref, send, recv, direction, jj, src).start()

    def finish_line(all_ref, send, recv):
        for t in range(nc):
            for direction, j in ((0, c - t), (1, c + t)):
                onward = (c + 1 < nc) if direction == 0 else (c >= 1)
                jj = jnp.clip(j, 0, nc - 1)

                @pl.when((j >= 0) & (j < nc) & onward)
                def _():
                    line(all_ref, send, recv, direction, jj, all_ref.at[jj]).wait_send()

    def pre_send(i, n):
        unit = r * nc + i
        user = unit % nr
        if n == nx - 1:
            target, first = mate_row, True
        else:
            first = user // 2 == peers[n]
            target = jnp.where(first, user, 2 * peers[n] + k)
        return remote(pre_ref.at[i], pre_all.at[unit], pre_s.at[i, n], pre_r.at[unit], {"row": target}), first

    def pre_unit(unit):
        source, user = unit // nc, unit % nr
        away = source // 2 != x
        straight = jnp.where(user // 2 == x, user == r, source % 2 == k)
        return away, away & straight, user == r

    def pre_relay(unit):
        return remote(pre_all.at[unit], pre_all.at[unit], pre_on.at[unit], pre_r.at[unit], mate)

    def pre_arrival(unit):
        pre_relay(unit).wait_recv()

    pass_on(cot_all, cot_s, cot_r, cot_ref, 0)
    for early in (True, False):
        for i in range(nc):
            for n in range(nx - 1) if early else (nx - 1,):
                copy, first = pre_send(i, n)
                if early:
                    pl.when(first)(copy.start)
                else:
                    copy.start()

    def pre_rest():
        for i in range(nc):
            for n in range(nx - 1):
                copy, first = pre_send(i, n)
                pl.when(jnp.logical_not(first))(copy.start)

    def pre_spread():
        def body(unit, _):
            away, straight, mine = pre_unit(unit)

            @pl.when(straight & jnp.logical_not(mine))
            def _():
                pre_arrival(unit)

            @pl.when(straight)
            def _():
                pre_relay(unit).start()
            return 0

        lax.fori_loop(0, nc * nr, body, 0)

    def activate_unit(unit):
        def body(i, _):
            at = pl.ds(pl.multiple_of(i * eb, eb), eb)
            act_all[unit, :, at] = gelu_value(pre_all[unit, :, at]).astype(BF16)
            return 0

        lax.fori_loop(0, hc // eb, body, 0)

    def activate_row(row, wait):
        def body(i, _):
            unit = row * nc + i
            if wait:
                pre_arrival(unit)
            activate_unit(unit)
            return 0

        lax.fori_loop(0, nc, body, 0)

    def activate_rest():
        def body(unit, _):
            away, straight, mine = pre_unit(unit)

            @pl.when(away & jnp.logical_not(straight))
            def _():
                pre_arrival(unit)

            @pl.when(away & jnp.logical_not(mine))
            def _():
                activate_unit(unit)
            return 0

        lax.fori_loop(0, nc * nr, body, 0)

    def s0(t):
        j = block_at(c, t, nc)
        if t == 0:
            local[0].wait()
            local[1].wait()
        block = cot_all[j]

        def body(i, _):
            at = pl.ds(pl.multiple_of(i * hb, hb), hb)
            got = lax.dot_general(block, down[at, :], LAST, preferred_element_type=F32)
            for s in range(nr):
                part[t, s, :, at] = got[s * ts : (s + 1) * ts]
            return 0

        lax.fori_loop(0, hc // hb, body, 0)
        for p in range(nx):
            h1_out[t, p] = part[t, 2 * p + (1 - k)].astype(BF16)
        started(remote(h1_out.at[t], h1_in.at[t], h1_s.at[t], h1_r.at[t], mate))

    def s1(t):
        remote(h1_out.at[t], h1_in.at[t], h1_s.at[t], h1_r.at[t], mate).wait_recv()
        for i, p in enumerate(peers):
            h2_out[t, i] = (part[t, 2 * p + k] + h1_in[t, p].astype(F32)).astype(BF16)
            started(remote(h2_out.at[t, i], h2_in.at[t, i], h2_s.at[t, i], h2_r.at[t, i],
                           {"row": 2 * p + k}))

    def pg_copy(t, index, source_row, target_row):
        unit = pg_all.at[block_at(c, t, nc) * nr + source_row]
        return remote(unit, unit, pg_s.at[t, index], pg_r.at[t, source_row], {"row": target_row})

    def s2(t):
        for i, p in enumerate(peers):
            remote(h2_out.at[t, i], h2_in.at[t, i], h2_s.at[t, i], h2_r.at[t, i],
                   {"row": 2 * p + k}).wait_recv()
        j = block_at(c, t, nc)
        unit = j * nr + r

        @pl.when((unit // nc) // 2 != x)
        def _():
            pre_arrival(unit)

        def body(i, _):
            at = pl.ds(pl.multiple_of(i * eb, eb), eb)
            total = part[t, 2 * x + k, :, at] + h1_in[t, x, :, at].astype(F32)
            for i in range(nx - 1):
                total += h2_in[t, i, :, at].astype(F32)
            value, slope = gelu_pair(pre_all[unit, :, at])
            act_all[unit, :, at] = value.astype(BF16)
            pg_all[unit, :, at] = (total * slope).astype(BF16)
            return 0

        lax.fori_loop(0, hc // eb, body, 0)
        for i, p in enumerate(peers):
            started(pg_copy(t, 1 + i, r, 2 * p + k))
        started(pg_copy(t, 0, r, mate_row))

    def s3(t):
        for i, p in enumerate(peers):
            pg_copy(t, 0, 2 * p + k, mate_row).wait_recv()
            started(pg_copy(t, nx + i, 2 * p + k, mate_row))

    outs = []

    def put_out(copy):
        copy.start()
        outs.append(copy)

    def pg_ready(t):
        for p in range(nx):
            pg_copy(t, 0, 2 * p + (1 - k), mate_row).wait_recv()
        units = pl.ds(block_at(c, t, nc) * nr, nr)
        put_out(pltpu.make_async_copy(pg_all.at[units], pg_out.at[units], pg_o.at[t]))

    def product(j, q):
        units = pg_all[pl.ds(j * nr, nr)]
        weight = up[q * dq : (q + 1) * dq, :]
        if ts % 16 == 0:
            return lax.dot_general(units.reshape(tb, hc), weight, LAST, preferred_element_type=F32)
        return jnp.concatenate(
            [lax.dot_general(units[s], weight, LAST, preferred_element_type=F32) for s in range(nr)], axis=0)

    def sum_copy(j, q):
        return remote(gi_out.at[j, q], gi_in.at[jnp.where(c + 1 == j, j, jnp.where(c - 1 == j, nc, j)), q],
                      gi_s.at[j, q], gi_r.at[jnp.where(c + 1 == j, j, jnp.where(c - 1 == j, nc, j)), q],
                      {"col": jnp.where(j > c, c + 1, c - 1)})

    def sum_arrival(slot, q):
        remote(gi_out.at[0, q], gi_in.at[slot, q], gi_s.at[0, q], gi_r.at[slot, q],
               {"col": jnp.where(c > 0, c - 1, c + 1)}).wait_recv()

    def sum_first(j, q):
        gi_out[j, q] = product(j, q).astype(BF16)
        sum_copy(j, q).start()

    def sum_onward(j, q):
        gi_acc[...] = product(j, q)
        sum_arrival(j, q)
        gi_out[j, q] = (gi_acc[...] + gi_in[j, q].astype(F32)).astype(BF16)
        sum_copy(j, q).start()

    def own_product():
        for q in range(nq):
            gi_own[q] = product(c, q)

    def own_sum(q):
        @pl.when(c > 0)
        def _():
            sum_arrival(c, q)
            gi_own[q] += gi_in[c, q].astype(F32)

        @pl.when(c < nc - 1)
        def _():
            sum_arrival(nc, q)
            gi_own[q] += gi_in[nc, q].astype(F32)

        gi_ref[:, q * dq : (q + 1) * dq] = gi_own[q].astype(BF16)

    def gd_copy(i):
        slot = i % 2
        return pltpu.make_async_copy(gd_buf.at[slot], gd_out.at[pl.ds(i * gb, gb)], gd_o.at[slot])

    def gd_tile(i):
        @pl.when(i >= 2)
        def _():
            gd_copy(i - 2).wait()

        tile = act_all[:, :, pl.ds(pl.multiple_of(i * gb, gb), gb)]
        if ts % 16 == 0:
            tile = tile.reshape(tb * nc, gb)
        else:
            tile = tile.astype(F32).reshape(tb * nc, gb).astype(BF16)
        gd_buf[i % 2] = lax.dot_general(
            tile, cot_all[...].reshape(tb * nc, dr), FIRST, preferred_element_type=F32) * token_scale
        gd_copy(i).start()

    def x_on(step):
        for direction, far in ((0, c), (1, nc - 1 - c)):
            t = step - far
            j = c - t if direction == 0 else c + t
            jj = jnp.clip(j, 0, nc - 1)
            fits = (t >= 0) & (t <= far) & (far < nc - 1)

            @pl.when(fits & (t > 0))
            def _():
                line(x_all, x_s, x_r, direction, jj, x_all.at[jj]).wait_recv()

            @pl.when(fits)
            def _():
                line(x_all, x_s, x_r, direction, jj, x_all.at[jj]).start()

    def x_put(j):
        return pltpu.make_async_copy(x_all.at[j], x_out.at[j], x_o.at[j])

    def x_rest():
        x_put(c).start()
        for direction, far in ((0, c), (1, nc - 1 - c)):
            for t in range(1, nc):
                j = c - t if direction == 0 else c + t
                jj = jnp.clip(j, 0, nc - 1)

                @pl.when((far == nc - 1))
                def _():
                    line(x_all, x_s, x_r, direction, jj, x_all.at[jj]).wait_recv()

                @pl.when((j >= 0) & (j < nc))
                def _():
                    x_put(jj).start()

    local[4].wait()
    for step in range(nc):
        if step == 1:
            local[3].wait()
        if step > 0:
            pass_on(cot_all, cot_s, cot_r, cot_ref, step)
        x_on(step)
        s0(step)
        if step == 0:
            local[2].wait()
            activate_row(r, False)
        s1(step)
        if step == 1:
            activate_row(mate_row, True)
        if step >= 1:
            s2(step - 1)
        if step >= 2:
            s3(step - 2)
    for t in range(nc - 2):
        pg_ready(t)
    own_product()
    s3(nc - 2)
    pg_ready(nc - 2)

    @pl.when(end)
    def _():
        def body(t, _):
            j = jnp.where(c == 0, t, nc - 1 - t)
            for q in range(nq):
                sum_first(j, q)
            return 0

        lax.fori_loop(1, nc - 1, body, 0)

    s2(nc - 1)
    pre_rest()
    for step in range(nc, 2 * nc - 3):
        x_on(step)
    s3(nc - 1)
    pg_ready(nc - 1)

    orders = visit_order(nc)
    tiles = hc // gb
    slots = 2 * nq
    share = -(-tiles // slots)

    def gd_some(slot):
        lo, hi = min(slot * share, tiles), min((slot + 1) * share, tiles)
        if hi - lo == 1:
            gd_tile(jnp.int32(lo))
        elif hi > lo:
            lax.fori_loop(lo, hi, lambda i, _: (gd_tile(i), 0)[1], 0)

    @pl.when(end)
    def _():
        j = jnp.where(c == 0, nc - 1, 0)
        for q in range(nq):
            sum_first(j, q)

    for n in range(nc - 2):
        @pl.when(jnp.logical_not(end))
        def _():
            j = pick([order[n] for order in orders], c)
            for q in range(nq):
                sum_onward(j, q)

    pre_spread()
    activate_rest()
    for q in range(nq):
        @pl.when(jnp.logical_not(end))
        def _():
            sum_onward(pick([order[nc - 2] for order in orders], c), q)

        gd_some(q)
    x_rest()
    for q in range(nq):
        own_sum(q)
        gd_some(nq + q)

    for copy in ends:
        copy.wait_send()
    for i in range(nc):
        for n in range(nx):
            pre_send(i, n)[0].wait_send()
    def relay_end(unit, _):
        pl.when(pre_unit(unit)[1])(pre_relay(unit).wait_send)
        return 0

    lax.fori_loop(0, nc * nr, relay_end, 0)

    def sum_end(j, _):
        @pl.when(j != c)
        def _():
            for q in range(nq):
                sum_copy(j, q).wait_send()
        return 0

    lax.fori_loop(0, nc, sum_end, 0)
    finish_line(cot_all, cot_s, cot_r)
    finish_line(x_all, x_s, x_r)
    for copy in outs:
        copy.wait()
    for j in range(nc):
        x_put(j).wait()
    for i in range(max(0, tiles - 2), tiles):
        gd_copy(i).wait()


def tail(x_ref, pg_ref, gd_in, gi_in, gu_ref, gd_ref, gi_ref):
    token_scale = 1.0 / math.sqrt(pg_ref.shape[0])
    gu_ref[...] = lax.dot_general(x_ref[...], pg_ref[...], FIRST, preferred_element_type=F32) * token_scale
    gd_ref[...] = gd_in[...]

    @pl.when(pl.program_id(0) == 0)
    def _():
        gi_ref[...] = gi_in[...]


def per_device(nr, nc, inputs, cotangent, preactivation, up_weight, down_weight):
    tb, dr = inputs.shape
    hc = up_weight.shape[1]
    ts, nx = tb // nr, nr // 2
    tokens = tb * nc
    dq, gb = min(256, dr), min(256, hc)
    nq = dr // dq
    dma = pltpu.SemaphoreType.DMA
    anywhere = pl.BlockSpec(memory_space=pl.ANY)
    shape = jax.ShapeDtypeStruct
    gi, x_all, pg_all, gd = pl.pallas_call(
        functools.partial(kernel, nr, nc),
        out_shape=(
            shape((tb, dr), BF16), shape((nc, tb, dr), BF16),
            shape((nc * nr, ts, hc), BF16), shape((hc, dr), F32),
        ),
        in_specs=[anywhere] * 5,
        out_specs=(pl.BlockSpec(memory_space=pltpu.VMEM),) + (anywhere,) * 3,
        scratch_shapes=[
            pltpu.VMEM((nc, tb, dr), BF16), pltpu.VMEM((nc, tb, dr), BF16),
            pltpu.VMEM((nc * nr, ts, hc), BF16), pltpu.VMEM((nc * nr, ts, hc), BF16),
            pltpu.VMEM((nc * nr, ts, hc), BF16),
            pltpu.VMEM(up_weight.shape, BF16), pltpu.VMEM(down_weight.shape, BF16),
            pltpu.VMEM((nc, nr, ts, hc), F32),
            pltpu.VMEM((nc, nx, ts, hc), BF16), pltpu.VMEM((nc, nx, ts, hc), BF16),
            pltpu.VMEM((nc, nx - 1, ts, hc), BF16), pltpu.VMEM((nc, nx - 1, ts, hc), BF16),
            pltpu.VMEM((nq, tb, dq), F32), pltpu.VMEM((tb, dq), F32),
            pltpu.VMEM((nc, nq, tb, dq), BF16), pltpu.VMEM((nc + 1, nq, tb, dq), BF16),
            pltpu.VMEM((2, gb, dr), F32),
            dma((5,)), dma((2, nc)), dma((nc,)), dma((2, nc)), dma((nc,)),
            dma((nc, nx)), dma((nc * nr,)), dma((nc * nr,)), dma((nc,)), dma((nc,)),
            dma((nc, nx - 1)), dma((nc, nx - 1)), dma((nc, 2 * nx)), dma((nc, nr)),
            dma((nc, nq)), dma((nc + 1, nq)),
            dma((nc,)), dma((nc,)), dma((2,)),
        ],
        compiler_params=pltpu.CompilerParams(
            collective_id=0, has_side_effects=True, vmem_limit_bytes=60 * 1024 * 1024
        ),
    )(inputs, cotangent, preactivation.reshape(nc, ts, hc), up_weight, down_weight)
    steps = dr // dq
    gb = hc // steps
    grad_up, grad_down, grad_input = pl.pallas_call(
        tail,
        grid=(steps,),
        out_shape=(shape((dr, hc), F32), shape((hc, dr), F32), shape((tb, dr), BF16)),
        in_specs=[
            pl.BlockSpec((tokens, dq), lambda i: (0, i)),
            pl.BlockSpec((tokens, hc), lambda i: (0, 0), pipeline_mode=pl.Buffered(1)),
            pl.BlockSpec((gb, dr), lambda i: (i, 0)),
            pl.BlockSpec((tb, dr), lambda i: (0, 0), pipeline_mode=pl.Buffered(1)),
        ],
        out_specs=(
            pl.BlockSpec((dq, hc), lambda i: (i, 0)),
            pl.BlockSpec((gb, dr), lambda i: (i, 0)),
            pl.BlockSpec((tb, dr), lambda i: (0, 0)),
        ),
        compiler_params=pltpu.CompilerParams(vmem_limit_bytes=48 * 1024 * 1024),
    )(x_all.reshape(tokens, dr), pg_all.reshape(tokens, hc), gd, gi)
    return (grad_input, grad_up, grad_down)


def solution(mesh):
    placed = (
        P(("groups", "col"), "row"),
        P(("groups", "col"), "row"),
        P(("groups", "row"), "col"),
        P("row", "col"),
        P("col", "row"),
    )
    return jax.shard_map(
        functools.partial(per_device, mesh.shape["row"], mesh.shape["col"]),
        mesh=mesh,
        in_specs=placed,
        out_specs=(
            P(("groups", "col"), "row"),
            P(("groups", "row"), "col"),
            P(("groups", "col"), "row"),
        ),
        check_vma=False,
    )
```

profile of v0, /device:TPU:0, one launch (start us, length us, event | category | flops | bytes accessed | tf_op | source)
XLA Modules:
  0.0 112.4 jit_solution(5025859904146205229)
XLA Ops:
  0.6 96.1 %shard_map.76 = (bf16[192,1024]{1,0:T(8,128)(2,1)}, bf16[4,192,1024]{2,1,0:T(8,128)(2,1)}, bf16[16,48,2048]{2,1,0:T(8,128)(2,1)}, f32[2048,1024]{1,0:T(8,128)}) custom-call(bf16[192,1024]{1,0:T(8,128)(2,1)} %x_ref.1, bf16[192,1024]{1,0:T(8,128)(2,1)} %cot_ref.1, bf16[4,48,2048]{2,1,0:T(8,128)(2,1)} %bitcast.5, bf16[1024,2048]{1,0:T(8,128)(2,1)} %up_ref.1, ...), custom_call_target="tpu_custom_call" | custom-call | tf_op jit(solution)/shard_map/pallas_call | solution.py:518
  96.8 0.0 copy-start
  96.8 1.9 %copy-done = bf16[16,48,2048]{2,1,0:T(8,128)(2,1)S(1)} copy-done((bf16[16,48,2048]{2,1,0:T(8,128)(2,1)S(1)}, bf16[16,48,2048]{2,1,0:T(8,128)(2,1)}, u32[]{:S(2)}) %copy-start) | copy-done | bytes 3145752
  98.7 0.0 copy-start.1
  98.7 1.4 %copy-done.1 = bf16[4,192,1024]{2,1,0:T(8,128)(2,1)S(1)} copy-done((bf16[4,192,1024]{2,1,0:T(8,128)(2,1)S(1)}, bf16[4,192,1024]{2,1,0:T(8,128)(2,1)}, u32[]{:S(2)}) %copy-start.1) | copy-done | bytes 1572888
  100.1 0.0 copy-start.2
  100.1 1.0 copy-done.2
  101.1 11.4 %shard_map.77 = (f32[1024,2048]{1,0:T(8,128)}, f32[2048,1024]{1,0:T(8,128)}, bf16[192,1024]{1,0:T(8,128)(2,1)}) custom-call(bf16[768,1024]{1,0:T(8,128)(2,1)S(1)} %bitcast.4, bf16[768,2048]{1,0:T(8,128)(2,1)S(1)} %bitcast.3, f32[2048,1024]{1,0:T(8,128)} %get-tuple-element.12.gd_in, bf16[192,1024]{1,0:T(8,128)(2,1)S(1)} %copy-done.2), custom_call_target="tpu_custom_call" | custom-call | tf_op jit(solution)/shard_map/pallas_call | solution.py:549
Async XLA Ops:
  96.8 1.9 %copy-start = (bf16[16,48,2048]{2,1,0:T(8,128)(2,1)S(1)}, bf16[16,48,2048]{2,1,0:T(8,128)(2,1)}, u32[]{:S(2)}) copy-start(bf16[16,48,2048]{2,1,0:T(8,128)(2,1)} %get-tuple-element.11) | copy-start | bytes 9437188
  98.7 1.4 %copy-start.1 = (bf16[4,192,1024]{2,1,0:T(8,128)(2,1)S(1)}, bf16[4,192,1024]{2,1,0:T(8,128)(2,1)}, u32[]{:S(2)}) copy-start(bf16[4,192,1024]{2,1,0:T(8,128)(2,1)} %get-tuple-element.10) | copy-start | bytes 4718596
  100.1 1.0 copy-start.2
where the time goes:
time: 113 us; the launch traced here: 112 us
  Pallas kernels  107 us (95%)
  local copies, waits for them, and re-layouts  4.29 us (4%)
    pallas_call x1, Pallas kernels, per_device(): pl.pallas_call(functools.partial(kernel, nr, nc), out_shape=(shape((tb, d...  96.1 us
    pallas_call x1, Pallas kernels, per_device(): pl.pallas_call(tail, grid=(steps,), out_shape=(shape((dr, hc), F32), shap...  11.4 us
    unnamed x6, local copies, waits for them, and re-layouts  4.29 us

commit v1 on v0

--- a/solution.py
+++ b/solution.py
@@ -44,12 +44,14 @@
     return value
 
 
-def visit_order(nc):
-    orders = []
+def sum_plan(nc, nq):
+    orders, events = [], []
     for c in range(nc):
-        far = [(j, c, j) if j > c else (nc - 1 - j, nc - 1 - c, j) for j in range(nc) if j != c]
-        orders.append([j for _, _, j in sorted(far)])
-    return orders
+        ranked = sorted((j, c, j) if j > c else (nc - 1 - j, nc - 1 - c, j) for j in range(nc) if j != c)
+        orders.append([j for _, _, j in ranked])
+        pieces = [(key, 2.2 * hops + q, n, q) for n, (key, hops, _) in enumerate(ranked) if n > 0 for q in range(nq)]
+        events.append([(n, q) for _, _, n, q in sorted(pieces)])
+    return orders, events
 
 
 def block_at(c, t, nc):
@@ -66,9 +68,9 @@
     gi_ref, x_out, pg_out, gd_out = rest[:4]
     (
     x_all, cot_all, pre_all, act_all, pg_all, up, down, part, h1_out, h1_in, h2_out, h2_in,
-    gi_own, gi_acc, gi_out, gi_in, gd_buf,
+    gi_own, gi_acc, gi_part, gi_out, gi_in, gd_buf,
     loc, cot_s, cot_r, x_s, x_r, pre_s, pre_on, pre_r, h1_s, h1_r, h2_s, h2_r, pg_s, pg_r, gi_s, gi_r,
-    x_o, pg_o, gd_o,
+    x_o, pg_o, gd_o, gi_o,
     ) = rest[4:]
     r, c = lax.axis_index("row"), lax.axis_index("col")
     nx = nr // 2
@@ -96,7 +98,7 @@
         pltpu.make_async_copy(up_ref, up, loc.at[3]),
         pltpu.make_async_copy(x_ref, x_all.at[c], loc.at[4]),
     ]
-    for copy in local:
+    for copy in local[:3]:
         copy.start()
     pl.semaphore_wait(barrier, nr + nc - 2)
 
@@ -310,7 +312,8 @@
                {"col": jnp.where(c > 0, c - 1, c + 1)}).wait_recv()
 
     def sum_first(j, q):
-        gi_out[j, q] = product(j, q).astype(BF16)
+        gi_acc[...] = product(j, q)
+        gi_out[j, q] = gi_acc[...].astype(BF16)
         sum_copy(j, q).start()
 
     def sum_onward(j, q):
@@ -334,7 +337,8 @@
             sum_arrival(nc, q)
             gi_own[q] += gi_in[nc, q].astype(F32)
 
-        gi_ref[:, q * dq : (q + 1) * dq] = gi_own[q].astype(BF16)
+        gi_out[c, q] = gi_own[q].astype(BF16)
+        put_out(pltpu.make_async_copy(gi_out.at[c, q], gi_ref.at[q], gi_o.at[q]))
 
     def gd_copy(i):
         slot = i % 2
@@ -387,84 +391,92 @@
                 def _():
                     x_put(jj).start()
 
-    local[4].wait()
+    def sum_near(t):
+        @pl.when(end)
+        def _():
+            for q in range(nq):
+                sum_first(jnp.where(c == 0, t, nc - 1 - t), q)
+
+    last = nc - 1
     for step in range(nc):
-        if step == 1:
-            local[3].wait()
         if step > 0:
             pass_on(cot_all, cot_s, cot_r, cot_ref, step)
-        x_on(step)
+            x_on(step - 1)
         s0(step)
         if step == 0:
+            local[3].start()
+            local[4].start()
             local[2].wait()
             activate_row(r, False)
         s1(step)
+        if step == 0:
+            local[3].wait()
+            local[4].wait()
         if step == 1:
             activate_row(mate_row, True)
-        if step >= 1:
-            s2(step - 1)
         if step >= 2:
-            s3(step - 2)
-    for t in range(nc - 2):
-        pg_ready(t)
-    own_product()
-    s3(nc - 2)
-    pg_ready(nc - 2)
-
-    @pl.when(end)
-    def _():
-        def body(t, _):
-            j = jnp.where(c == 0, t, nc - 1 - t)
-            for q in range(nq):
-                sum_first(j, q)
-            return 0
-
-        lax.fori_loop(1, nc - 1, body, 0)
-
-    s2(nc - 1)
+            s3(step - 1)
+            pg_ready(step - 1)
+            sum_near(step - 1)
+        if 1 <= step < last:
+            s2(step)
+    x_on(last)
+    s2(last)
+    s2(0)
     pre_rest()
     for step in range(nc, 2 * nc - 3):
         x_on(step)
-    s3(nc - 1)
-    pg_ready(nc - 1)
-
-    orders = visit_order(nc)
-    tiles = hc // gb
-    slots = 2 * nq
-    share = -(-tiles // slots)
-
-    def gd_some(slot):
-        lo, hi = min(slot * share, tiles), min((slot + 1) * share, tiles)
-        if hi - lo == 1:
-            gd_tile(jnp.int32(lo))
-        elif hi > lo:
-            lax.fori_loop(lo, hi, lambda i, _: (gd_tile(i), 0)[1], 0)
-
-    @pl.when(end)
-    def _():
-        j = jnp.where(c == 0, nc - 1, 0)
-        for q in range(nq):
-            sum_first(j, q)
-
-    for n in range(nc - 2):
+    orders, events = sum_plan(nc, nq)
+
+    def pass_first():
         @pl.when(jnp.logical_not(end))
         def _():
+            j = pick([order[0] for order in orders], c)
+            for q in range(nq):
+                sum_onward(j, q)
+
+    def pass_later(lo, hi):
+        for e in range(lo, hi):
+            @pl.when(jnp.logical_not(end))
+            def _():
+                n, q = (pick([plan[e][at] for plan in events], c) for at in (0, 1))
+                j = pick([order[plan[e][0]] for order, plan in zip(orders, events)], c)
+                sum_arrival(j, q)
+                gi_out[j, q] = (gi_part[n - 1, q] + gi_in[j, q].astype(F32)).astype(BF16)
+                sum_copy(j, q).start()
+
+    if nc > 3:
+        pass_first()
+    s3(last)
+    pg_ready(last)
+    sum_near(last)
+    if nc == 3:
+        pass_first()
+
+    @pl.when(jnp.logical_not(end))
+    def _():
+        for n in range(1, nc - 1):
             j = pick([order[n] for order in orders], c)
             for q in range(nq):
-                sum_onward(j, q)
-
+                gi_part[n - 1, q] = product(j, q)
+
+    count = len(events[0])
+    pass_later(0, count // 4)
+    s3(0)
+    pg_ready(0)
+    own_product()
+    pass_later(count // 4, 3 * count // 4)
     pre_spread()
     activate_rest()
+    x_rest()
+    pass_later(3 * count // 4, count)
+    tiles = hc // gb
+    share = -(-tiles // nq)
     for q in range(nq):
-        @pl.when(jnp.logical_not(end))
-        def _():
-            sum_onward(pick([order[nc - 2] for order in orders], c), q)
-
-        gd_some(q)
-    x_rest()
-    for q in range(nq):
+        lo, hi = min(q * share, tiles), min((q + 1) * share, tiles)
+        if hi > lo:
+            lax.fori_loop(lo, hi, lambda i, _: (gd_tile(i), 0)[1], 0)
         own_sum(q)
-        gd_some(nq + q)
 
     for copy in ends:
         copy.wait_send()
@@ -495,14 +507,36 @@
         gd_copy(i).wait()
 
 
-def tail(x_ref, pg_ref, gd_in, gi_in, gu_ref, gd_ref, gi_ref):
+def tail(x_ref, pg_ref, gd_in, gi_in, gu_ref, gd_ref, gi_ref, x, pg, gu, gd, gi, loads, gd_loads, stores):
     token_scale = 1.0 / math.sqrt(pg_ref.shape[0])
-    gu_ref[...] = lax.dot_general(x_ref[...], pg_ref[...], FIRST, preferred_element_type=F32) * token_scale
-    gd_ref[...] = gd_in[...]
-
-    @pl.when(pl.program_id(0) == 0)
-    def _():
-        gi_ref[...] = gi_in[...]
+    parts, tokens, cols = pg.shape
+    blocks, rows = gd.shape[:2]
+    nq, dq = gi_in.shape[0], gi_in.shape[2]
+    read = pltpu.make_async_copy
+    x_load = read(x_ref, x, loads.at[parts])
+    pg_load = [read(pg_ref.at[:, pl.ds(n * cols, cols)], pg.at[n], loads.at[n]) for n in range(parts)]
+    gi_load = read(gi_in, gi, loads.at[parts + 1])
+    gd_load = [read(gd_in.at[pl.ds(n * rows, rows)], gd.at[n], gd_loads.at[n]) for n in range(blocks)]
+    gu_store = [read(gu.at[n], gu_ref.at[:, pl.ds(n * cols, cols)], stores.at[n]) for n in range(parts)]
+    gi_store = [read(gi.at[q], gi_ref.at[:, pl.ds(q * dq, dq)], loads.at[q]) for q in range(nq)]
+    gd_store = [read(gd.at[n], gd_ref.at[pl.ds(n * rows, rows)], gd_loads.at[n]) for n in range(blocks)]
+    x_load.start()
+    for copy in pg_load + gd_load + [gi_load]:
+        copy.start()
+    x_load.wait()
+    each = -(-blocks // parts)
+    for n in range(parts):
+        pg_load[n].wait()
+        gu[n] = lax.dot_general(x[...], pg[n], FIRST, preferred_element_type=F32) * token_scale
+        gu_store[n].start()
+        for m in range(n * each, min((n + 1) * each, blocks)):
+            gd_load[m].wait()
+            gd_store[m].start()
+    gi_load.wait()
+    for copy in gi_store:
+        copy.start()
+    for copy in gu_store + gd_store + gi_store:
+        copy.wait()
 
 
 def per_device(nr, nc, inputs, cotangent, preactivation, up_weight, down_weight):
@@ -515,53 +549,50 @@
     dma = pltpu.SemaphoreType.DMA
     anywhere = pl.BlockSpec(memory_space=pl.ANY)
     shape = jax.ShapeDtypeStruct
+    scratch = [
+        pltpu.VMEM((nc, tb, dr), BF16), pltpu.VMEM((nc, tb, dr), BF16),
+        pltpu.VMEM((nc * nr, ts, hc), BF16), pltpu.VMEM((nc * nr, ts, hc), BF16),
+        pltpu.VMEM((nc * nr, ts, hc), BF16),
+        pltpu.VMEM(up_weight.shape, BF16), pltpu.VMEM(down_weight.shape, BF16),
+        pltpu.VMEM((nc, nr, ts, hc), F32),
+        pltpu.VMEM((nc, nx, ts, hc), BF16), pltpu.VMEM((nc, nx, ts, hc), BF16),
+        pltpu.VMEM((nc, nx - 1, ts, hc), BF16), pltpu.VMEM((nc, nx - 1, ts, hc), BF16),
+        pltpu.VMEM((nq, tb, dq), F32), pltpu.VMEM((tb, dq), F32), pltpu.VMEM((nc - 2, nq, tb, dq), F32),
+        pltpu.VMEM((nc, nq, tb, dq), BF16), pltpu.VMEM((nc + 1, nq, tb, dq), BF16),
+        pltpu.VMEM((2, gb, dr), F32),
+        dma((5,)), dma((2, nc)), dma((nc,)), dma((2, nc)), dma((nc,)),
+        dma((nc, nx)), dma((nc * nr,)), dma((nc * nr,)), dma((nc,)), dma((nc,)),
+        dma((nc, nx - 1)), dma((nc, nx - 1)), dma((nc, 2 * nx)), dma((nc, nr)),
+        dma((nc, nq)), dma((nc + 1, nq)),
+        dma((nc,)), dma((nc,)), dma((2,)), dma((nq,)),
+    ]
     gi, x_all, pg_all, gd = pl.pallas_call(
         functools.partial(kernel, nr, nc),
         out_shape=(
-            shape((tb, dr), BF16), shape((nc, tb, dr), BF16),
+            shape((nq, tb, dq), BF16), shape((nc, tb, dr), BF16),
             shape((nc * nr, ts, hc), BF16), shape((hc, dr), F32),
         ),
         in_specs=[anywhere] * 5,
-        out_specs=(pl.BlockSpec(memory_space=pltpu.VMEM),) + (anywhere,) * 3,
-        scratch_shapes=[
-            pltpu.VMEM((nc, tb, dr), BF16), pltpu.VMEM((nc, tb, dr), BF16),
-            pltpu.VMEM((nc * nr, ts, hc), BF16), pltpu.VMEM((nc * nr, ts, hc), BF16),
-            pltpu.VMEM((nc * nr, ts, hc), BF16),
-            pltpu.VMEM(up_weight.shape, BF16), pltpu.VMEM(down_weight.shape, BF16),
-            pltpu.VMEM((nc, nr, ts, hc), F32),
-            pltpu.VMEM((nc, nx, ts, hc), BF16), pltpu.VMEM((nc, nx, ts, hc), BF16),
-            pltpu.VMEM((nc, nx - 1, ts, hc), BF16), pltpu.VMEM((nc, nx - 1, ts, hc), BF16),
-            pltpu.VMEM((nq, tb, dq), F32), pltpu.VMEM((tb, dq), F32),
-            pltpu.VMEM((nc, nq, tb, dq), BF16), pltpu.VMEM((nc + 1, nq, tb, dq), BF16),
-            pltpu.VMEM((2, gb, dr), F32),
-            dma((5,)), dma((2, nc)), dma((nc,)), dma((2, nc)), dma((nc,)),
-            dma((nc, nx)), dma((nc * nr,)), dma((nc * nr,)), dma((nc,)), dma((nc,)),
-            dma((nc, nx - 1)), dma((nc, nx - 1)), dma((nc, 2 * nx)), dma((nc, nr)),
-            dma((nc, nq)), dma((nc + 1, nq)),
-            dma((nc,)), dma((nc,)), dma((2,)),
-        ],
+        out_specs=(anywhere,) * 4,
+        scratch_shapes=scratch,
         compiler_params=pltpu.CompilerParams(
             collective_id=0, has_side_effects=True, vmem_limit_bytes=60 * 1024 * 1024
         ),
     )(inputs, cotangent, preactivation.reshape(nc, ts, hc), up_weight, down_weight)
-    steps = dr // dq
-    gb = hc // steps
+    cols, rows = min(512, hc), min(256, hc)
+    parts, blocks = hc // cols, hc // rows
     grad_up, grad_down, grad_input = pl.pallas_call(
         tail,
-        grid=(steps,),
         out_shape=(shape((dr, hc), F32), shape((hc, dr), F32), shape((tb, dr), BF16)),
-        in_specs=[
-            pl.BlockSpec((tokens, dq), lambda i: (0, i)),
-            pl.BlockSpec((tokens, hc), lambda i: (0, 0), pipeline_mode=pl.Buffered(1)),
-            pl.BlockSpec((gb, dr), lambda i: (i, 0)),
-            pl.BlockSpec((tb, dr), lambda i: (0, 0), pipeline_mode=pl.Buffered(1)),
+        in_specs=[anywhere] * 4,
+        out_specs=(anywhere,) * 3,
+        scratch_shapes=[
+            pltpu.VMEM((tokens, dr), BF16), pltpu.VMEM((parts, tokens, cols), BF16),
+            pltpu.VMEM((parts, dr, cols), F32), pltpu.VMEM((blocks, rows, dr), F32),
+            pltpu.VMEM((nq, tb, dq), BF16),
+            dma((max(parts + 2, nq),)), dma((blocks,)), dma((parts,)),
         ],
-        out_specs=(
-            pl.BlockSpec((dq, hc), lambda i: (i, 0)),
-            pl.BlockSpec((gb, dr), lambda i: (i, 0)),
-            pl.BlockSpec((tb, dr), lambda i: (0, 0)),
-        ),
-        compiler_params=pltpu.CompilerParams(vmem_limit_bytes=48 * 1024 * 1024),
+        compiler_params=pltpu.CompilerParams(vmem_limit_bytes=60 * 1024 * 1024),
     )(x_all.reshape(tokens, dr), pg_all.reshape(tokens, hc), gd, gi)
     return (grad_input, grad_up, grad_down)
 

time: 113 us -> 88 us (0.78)
  Pallas kernels: 107 us -> 87 us
  local copies, waits for them, and re-layouts: 4.29 us -> 0 us
    pallas_call x2, Pallas kernels: 107 us -> 87 us  [the longest x1 77.4 us: per_device(): pl.pallas_call(functools.partial(kernel, nr, nc), out_shape=(shape((nq, t...]
    unnamed x6 -> x0, local copies, waits for them, and re-layouts: 4.29 us -> none
where the time goes in v1:
time: 88 us; the launch traced here: 87.8 us
  Pallas kernels  87 us (99%)
    pallas_call x1, Pallas kernels, per_device(): pl.pallas_call(functools.partial(kernel, nr, nc), out_shape=(shape((nq, t...  77.4 us
    pallas_call x1, Pallas kernels, per_device(): pl.pallas_call(tail, out_shape=(shape((dr, hc), F32), shape((hc, dr), F32...  9.62 us

profile of v1, /device:TPU:0, one launch (start us, length us, event | category | flops | bytes accessed | tf_op | source)
XLA Modules:
  0.0 87.8 jit_solution(8085436377237772247)
XLA Ops:
  0.6 77.4 %shard_map.76 = (bf16[4,192,256]{2,1,0:T(8,128)(2,1)}, bf16[4,192,1024]{2,1,0:T(8,128)(2,1)}, bf16[16,48,2048]{2,1,0:T(8,128)(2,1)}, f32[2048,1024]{1,0:T(8,128)}) custom-call(bf16[192,1024]{1,0:T(8,128)(2,1)} %x_ref.1, bf16[192,1024]{1,0:T(8,128)(2,1)} %cot_ref.1, bf16[4,48,2048]{2,1,0:T(8,128)(2,1)} %bitcast.5, bf16[1024,2048]{1,0:T(8,128)(2,1)} %up_ref.1, ...), custom_call_target="tpu_custom_call" | custom-call | tf_op jit(solution)/shard_map/pallas_call | solution.py:569
  78.0 9.6 %shard_map.77 = (f32[1024,2048]{1,0:T(8,128)}, f32[2048,1024]{1,0:T(8,128)}, bf16[192,1024]{1,0:T(8,128)(2,1)}) custom-call(bf16[768,1024]{1,0:T(8,128)(2,1)} %bitcast.4, bf16[768,2048]{1,0:T(8,128)(2,1)} %bitcast.3, f32[2048,1024]{1,0:T(8,128)} %get-tuple-element.12.gd_in, bf16[4,192,256]{2,1,0:T(8,128)(2,1)} %get-tuple-element.13.gi_in), custom_call_target="tpu_custom_call" | custom-call | tf_op jit(solution)/shard_map/pallas_call | solution.py:584
